TPU v7x, 512 devices: a whole 4x4x16 slice. The times are simulated.
512 devices in a mesh: row: 16 (over z_hi, y, core), col: 32 (over z_lo, x).
Axes of the slice: x: 4, y: 4, z: 16 (z_hi: 2, z_lo: 8; z = z_hi * 8 + z_lo), core: 2. Of those that a mesh axis runs over, the one named last changes fastest.
Arguments:
- query_grads: bfloat16 [256, 8192], P('row', 'col'), may hold values from -6 to 6
- query_acts: bfloat16 [256, 8192], P('col', 'row'), may hold values from -6 to 6
- train_grads: bfloat16 [512, 8192], P('row', 'col'), may hold values from -6 to 6
- train_acts: bfloat16 [512, 8192], P('col', 'row'), may hold values from -6 to 6
- grad_basis: bfloat16 [8192, 8192], P('col', 'row'), may hold values from -0.0625 to 0.0625
- act_basis: bfloat16 [8192, 8192], P('row', 'col'), may hold values from -0.0625 to 0.0625
- eigen_corr: float32 [8192, 8192], P('row', 'col'), may hold values from 0.02 to 2
- damping: float32 [], replicated, may hold values from 0.05 to 0.5
- query_seq: int32 [256], replicated, may hold values from 0 to 31, never falling along the last dimension, each value on 1 to 16 neighbouring positions
- train_doc: int32 [512], replicated, may hold values from 0 to 15, never falling along the last dimension, each value on 1 to 64 neighbouring positions
Outputs:
- scores: float32 [32, 512], P(None, 'col')
- doc_scores: float32 [32, 16], replicated
Inputs may be any that keep to these rules, and one draw needn't show every extreme that they name: `query_seq`: Non-decreasing along the query tokens; every sequence has 1 to 16 tokens, and one has exactly that many. `train_doc`: Non-decreasing along the training tokens; every document has 1 to 64 tokens, and one has exactly that many.
All inputs are finite; a program needn't handle non-finite values.
Results may differ from a plain program's by a relative error of at most 0.005.
Values may be sent and summed in bfloat16 or wider, within the bound.
No kernel may reach another device: no remote copies, remote signals or barrier semaphores. Data moves between devices by JAX's collectives and lax.ppermute only.
A program may use at most 64 MiB of HBM per device.

v0:
```python
import jax
import jax.numpy as jnp
from jax import lax
from jax.sharding import PartitionSpec as P

D = 8192
S = 32
DOCS = 16


def local(
    query_grads,
    query_acts,
    train_grads,
    train_acts,
    grad_basis,
    act_basis,
    eigen_corr,
    damping,
    query_seq,
    train_doc,
):
    grad_query, grad_train = (
        lax.all_gather(query_grads, "row", axis=0, tiled=True),
        lax.all_gather(train_grads, "row", axis=0, tiled=True),
    )
    act_query, act_train = (
        lax.all_gather(query_acts, "col", axis=0, tiled=True),
        lax.all_gather(train_acts, "col", axis=0, tiled=True),
    )
    grads_all = jnp.concatenate([grad_query, grad_train], axis=0)
    acts_all = jnp.concatenate([act_query, act_train], axis=0)
    n_query = grad_query.shape[0]
    grad_part = jnp.dot(grads_all, grad_basis, preferred_element_type=jnp.float32)
    grads_rot = lax.psum(grad_part, "col").astype(jnp.bfloat16)
    act_part = jnp.dot(acts_all, act_basis, preferred_element_type=jnp.float32)
    acts_rot = lax.psum(act_part, "row").astype(jnp.bfloat16)
    rot_gq = grads_rot[:n_query]
    rot_gu = grads_rot[n_query:]
    rot_aq = acts_rot[:n_query]
    rot_au = acts_rot[n_query:]
    denom = eigen_corr + damping
    act_wide = rot_au.astype(jnp.float32)
    row_block = eigen_corr.shape[0]
    col_block = eigen_corr.shape[1]
    group = 4

    def score_group(first):
        seq_ids = first + jnp.arange(group, dtype=jnp.int32)
        member = (query_seq[:, None] == seq_ids[None, :]).astype(jnp.bfloat16)
        weighted = (member[:, :, None] * rot_gq[:, None, :]).reshape(n_query, group * row_block)
        outer = lax.dot_general(
            weighted, rot_aq, (((0,), (0,)), ((), ())), preferred_element_type=jnp.float32
        )
        precond = (outer.reshape(group, row_block, col_block) / denom[None, :, :]).astype(
            jnp.bfloat16
        )
        mapped = jnp.einsum("ui,sij->usj", rot_gu, precond, preferred_element_type=jnp.float32)
        return jnp.sum(mapped * act_wide[:, None, :], axis=2).T

    starts = jnp.arange(S // group, dtype=jnp.int32) * group
    partial_scores = lax.map(score_group, starts).reshape(S, rot_gu.shape[0]) / D
    doc_table = (train_doc[:, None] == jnp.arange(DOCS, dtype=jnp.int32)[None, :]).astype(
        jnp.float32
    )
    counts = jnp.sum(doc_table, axis=0)
    owned = rot_gu.shape[0] // lax.axis_size("col")
    first_owned = lax.axis_index("col") * owned
    totals = lax.psum(partial_scores, ("row", "col"))
    scores = lax.dynamic_slice_in_dim(totals, first_owned, owned, 1)
    doc_sum = jnp.dot(totals, doc_table, precision=lax.Precision.HIGHEST)
    return (scores, doc_sum / counts[None, :])


def solution(mesh):
    in_specs = (
        P("row", "col"),
        P("col", "row"),
        P("row", "col"),
        P("col", "row"),
        P("col", "row"),
        P("row", "col"),
        P("row", "col"),
        P(),
        P(),
        P(),
    )
    out_specs = (P(None, "col"), P())
    return jax.shard_map(local, mesh=mesh, in_specs=in_specs, out_specs=out_specs, check_vma=False)
```

profile of v0, /device:TPU:1, one launch (start us, length us, event | category | flops | bytes accessed | tf_op | source)
XLA Modules:
  0.0 1171.2 jit_solution(7079369166472949300)
XLA Ops:
  7.2 52.0 %all_gather.13 = bf16[512,256]{1,0:T(8,128)(2,1)S(1)} all-gather(bf16[32,256]{1,0:T(8,128)(2,1)} %param.14), channel_id=1, replica_groups=mesh['row'=16,'col'=32] {'row'}, dimensions={0}, use_global_device_ids=true | all-gather | bytes 278528 | tf_op jit(solution)/shard_map/all_gather | solution.py:25
  59.2 34.3 %all_gather.12 = bf16[256,256]{1,0:T(8,128)(2,1)S(1)} all-gather(bf16[16,256]{1,0:T(8,128)(2,1)} %param.12), channel_id=1, replica_groups=mesh['row'=16,'col'=32] {'row'}, dimensions={0}, use_global_device_ids=true | all-gather | bytes 139264 | tf_op jit(solution)/shard_map/all_gather | solution.py:24
  93.5 0.4 fusion.16
  93.9 219.5 %all-reduce.5 = bf16[768,512]{1,0:T(8,128)(2,1)S(1)} all-reduce(f32[768,512]{1,0:T(8,128)S(1)} %fusion.16), channel_id=1, replica_groups=mesh['row'=16,'col'=32] {'col'}, use_global_device_ids=true, to_apply=%region_0.0 | all-reduce | flops 393216 | bytes 2359296 | tf_op jit(solution)/shard_map/psum | solution.py:35
  313.4 100.8 %all_gather.15 = bf16[512,512]{1,0:T(8,128)(2,1)S(1)} all-gather(bf16[16,512]{1,0:T(8,128)(2,1)S(1)} %copy-done.4), channel_id=1, replica_groups=mesh['row'=16,'col'=32] {'col'}, dimensions={0}, use_global_device_ids=true | all-gather | bytes 540672 | tf_op jit(solution)/shard_map/all_gather | solution.py:29
  414.2 100.0 %all_gather.14 = bf16[256,512]{1,0:T(8,128)(2,1)S(1)} all-gather(bf16[8,512]{1,0:T(8,128)(2,1)S(1)} %copy-done.5), channel_id=1, replica_groups=mesh['row'=16,'col'=32] {'col'}, dimensions={0}, use_global_device_ids=true | all-gather | bytes 270336 | tf_op jit(solution)/shard_map/all_gather | solution.py:28
  514.2 0.4 fusion.12
  514.6 176.3 %all-reduce.6 = bf16[768,256]{1,0:T(8,128)(2,1)S(1)} all-reduce(f32[768,256]{1,0:T(8,128)S(1)} %fusion.12), channel_id=1, replica_groups=mesh['row'=16,'col'=32] {'row'}, use_global_device_ids=true, to_apply=%region_1.0 | all-reduce | flops 196608 | bytes 1179648 | tf_op jit(solution)/shard_map/psum | solution.py:37
  691.0 0.1 copy.19
  691.1 0.2 copy.20
  692.1 19.3 %while.10 = (s32[]{:T(128)}, f32[8,4,512]{2,1,0:T(4,128)S(1)}, s32[256]{0:T(256)S(1)}, s32[8]{0:T(128)S(1)}, bf16[256,512]{0,1:T(8,128)(2,1)S(1)}, /*index=5*/bf...) while((s32[]{:T(128)}, f32[8,4,512]{2,1,0:T(4,128)S(1)}, ...), condition=%wide.region_4.5_spmd, body=%wide.region_2.4_spmd.sunk | while | flops 807927808 | bytes 1995929 | solution.py:62
  692.1 0.6 dynamic_slice.10
  692.7 0.6 iota_add_fusion.2
  693.3 0.1 compare_convert_fusion.2
  693.4 1.1 fusion.33
  694.5 0.6 dynamic_slice.10
  695.1 0.6 iota_add_fusion.2
  695.8 1.1 fusion.33
  696.9 0.6 dynamic_slice.10
  697.5 0.6 iota_add_fusion.2
  698.2 0.1 compare_convert_fusion.2
  698.2 1.1 fusion.33
  699.3 0.6 dynamic_slice.10
  699.9 0.6 iota_add_fusion.2
  700.6 0.1 compare_convert_fusion.2
  700.7 1.1 fusion.33
  701.8 0.6 dynamic_slice.10
  702.4 0.6 iota_add_fusion.2
  703.0 0.1 compare_convert_fusion.2
  703.1 1.1 fusion.33
  704.2 0.6 dynamic_slice.10
  704.8 0.6 iota_add_fusion.2
  705.4 0.1 compare_convert_fusion.2
  705.5 1.1 fusion.33
  706.6 0.6 dynamic_slice.10
  707.2 0.6 iota_add_fusion.2
  707.8 0.1 compare_convert_fusion.2
  707.9 1.1 fusion.33
  709.0 0.6 dynamic_slice.10
  709.6 0.6 iota_add_fusion.2
  710.3 0.1 compare_convert_fusion.2
  710.3 1.1 fusion.33
  711.5 0.6 div.26
  712.1 0.1 convert_reduce_fusion
  712.2 449.1 %all-reduce.4.cloned.1.call-done = f32[32,512]{1,0:T(8,128)} async-done(((f32[32,512]{1,0:T(8,128)}), f32[32,512]{1,0:T(8,128)}) %all-reduce.4.cloned.1.call-update) | async-done | bytes 65552 | tf_op jit(solution)/shard_map/psum | solution.py:69
  1161.3 0.8 constant_dynamic-slice_fusion
  1162.1 0.7 copy.21
  1162.8 1.6 convolution_divide_fusion
  (36 shorter events, 0.5 us)
Async XLA Ops:
  7.2 86.4 %copy-start = (bf16[256,512]{1,0:T(8,128)(2,1)S(1)}, bf16[256,512]{1,0:T(8,128)(2,1)}, u32[]{:S(2)}) copy-start(bf16[256,512]{1,0:T(8,128)(2,1)} %param.16) | copy-start | bytes 786436
  7.2 1154.2 %all-reduce.4.cloned.1.call-start = ((), (), s32[]{:S(2)}) async-start(), calls=%async_computation | async-start | bytes 131072 | tf_op jit(solution)/shard_map/psum | solution.py:69
  93.9 219.6 %copy-start.4 = (bf16[16,512]{1,0:T(8,128)(2,1)S(1)}, bf16[16,512]{1,0:T(8,128)(2,1)}, u32[]{:S(2)}) copy-start(bf16[16,512]{1,0:T(8,128)(2,1)} %param.15) | copy-start | bytes 49156
  313.4 201.2 %copy-start.1 = (bf16[768,512]{1,0:T(8,128)(2,1)}, bf16[768,512]{1,0:T(8,128)(2,1)S(1)}, u32[]{:S(2)}) copy-start(bf16[768,512]{1,0:T(8,128)(2,1)S(1)} %all-reduce.5) | copy-start | bytes 2359300
  313.4 100.8 %copy-start.5 = (bf16[8,512]{1,0:T(8,128)(2,1)S(1)}, bf16[8,512]{1,0:T(8,128)(2,1)}, u32[]{:S(2)}) copy-start(bf16[8,512]{1,0:T(8,128)(2,1)} %param.13) | copy-start | bytes 24580
  313.4 200.8 %copy-start.7 = (bf16[512,256]{1,0:T(8,128)(2,1)S(1)}, bf16[512,256]{1,0:T(8,128)(2,1)}, u32[]{:S(2)}) copy-start(bf16[512,256]{1,0:T(8,128)(2,1)} %param.17) | copy-start | bytes 786436
  690.9 1.1 copy-start.2
  690.9 1.2 slice-start
  690.9 1.2 copy-start.3
  692.1 20.0 %copy-start.6 = (s32[512]{0:T(512)S(1)}, s32[512]{0:T(512)}, u32[]{:S(2)}) copy-start(s32[512]{0:T(512)} %param.21) | copy-start | bytes 6148
Sparse Core Ops, SparseCore 0:
  712.2 449.0 all-reduce.3
where the time goes:
time: 1170 us
  blocking collectives  683 us (58%)
  waiting for transfers between devices  449 us (38%)
  between operations  14.9 us (1%)
    psum x1, waiting for transfers between devices, local(): totals = lax.psum(partial_scores, ('row', 'col'))  449 us
    psum x1, blocking collectives, local(): grads_rot = lax.psum(grad_part, 'col').astype(jnp.bfloat16)  219 us
    psum x1, blocking collectives, local(): acts_rot = lax.psum(act_part, 'row').astype(jnp.bfloat16)  176 us
    all_gather x1, blocking collectives, local(): lax.all_gather(train_acts, 'col', axis=0, tiled=True)  101 us
    all_gather x1, blocking collectives, local(): lax.all_gather(query_acts, 'col', axis=0, tiled=True)  100 us
    all_gather x1, blocking collectives, local(): lax.all_gather(train_grads, 'row', axis=0, tiled=True)  52 us
    all_gather x1, blocking collectives, local(): lax.all_gather(query_grads, 'row', axis=0, tiled=True)  34.3 us
  transfers between devices with their start and end apart: 1, of which 1 were waited for; matrix products, arithmetic and copies ran while one was open for 0% of the time, Pallas kernels for 0%

commit v1 on v0

--- a/solution.py
+++ b/solution.py
@@ -6,6 +6,12 @@
 D = 8192
 S = 32
 DOCS = 16
+
+
+def add_all(array, mesh_axis):
+    shards = lax.all_gather(array, mesh_axis, axis=0, tiled=False)
+    total = shards.sum(axis=0)
+    return total
 
 
 def local(
@@ -32,7 +38,7 @@
     acts_all = jnp.concatenate([act_query, act_train], axis=0)
     n_query = grad_query.shape[0]
     grad_part = jnp.dot(grads_all, grad_basis, preferred_element_type=jnp.float32)
-    grads_rot = lax.psum(grad_part, "col").astype(jnp.bfloat16)
+    grads_rot = add_all(grad_part, "col").astype(jnp.bfloat16)
     act_part = jnp.dot(acts_all, act_basis, preferred_element_type=jnp.float32)
     acts_rot = lax.psum(act_part, "row").astype(jnp.bfloat16)
     rot_gq = grads_rot[:n_query]

time: 1170 us -> 1260 us (1.077)
  waiting for transfers between devices: 449 us -> 732 us
  blocking collectives: 683 us -> 467 us
  other arithmetic: 5.97 us -> 23.9 us
    psum x1 -> x0, blocking collectives: 219 us -> none  [local(): grads_rot = lax.psum(grad_part, 'col').astype(jnp.bfloat16)]
    all_gather x0 -> x1, waiting for transfers between devices: none -> 180 us  [add_all(): shards = lax.all_gather(array, mesh_axis, axis=0, tiled=False)]
    psum x1, waiting for transfers between devices: 449 us -> 552 us  [local(): totals = lax.psum(partial_scores, ('row', 'col'))]
    psum x1, blocking collectives: 176 us -> 152 us  [local(): acts_rot = lax.psum(act_part, 'row').astype(jnp.bfloat16)]
    reduce_sum x0 -> x1, other arithmetic: none -> 18 us  [add_all(): total = shards.sum(axis=0)]
    all_gather x1, blocking collectives: 100 us -> 114 us  [local(): lax.all_gather(query_acts, 'col', axis=0, tiled=True)]
    all_gather x1, blocking collectives: 101 us -> 114 us  [local(): lax.all_gather(train_acts, 'col', axis=0, tiled=True)]
  transfers between devices with their start and end apart: 1 -> 2, of which waited for: 1 -> 2; matrix products, arithmetic and copies ran while one was open for 0% -> 0% of each run, Pallas kernels for 0% -> 0%
where the time goes in v1:
time: 1260 us
  waiting for transfers between devices  732 us (58%)
  blocking collectives  467 us (37%)
  other arithmetic  23.9 us (2%)
  between operations  14.9 us (1%)
    psum x1, waiting for transfers between devices, local(): totals = lax.psum(partial_scores, ('row', 'col'))  552 us
    all_gather x1, waiting for transfers between devices, add_all(): shards = lax.all_gather(array, mesh_axis, axis=0, tiled=False)  180 us
    psum x1, blocking collectives, local(): acts_rot = lax.psum(act_part, 'row').astype(jnp.bfloat16)  152 us
    all_gather x1, blocking collectives, local(): lax.all_gather(train_acts, 'col', axis=0, tiled=True)  114 us
    all_gather x1, blocking collectives, local(): lax.all_gather(query_acts, 'col', axis=0, tiled=True)  114 us
    all_gather x1, blocking collectives, local(): lax.all_gather(train_grads, 'row', axis=0, tiled=True)  52 us
    all_gather x1, blocking collectives, local(): lax.all_gather(query_grads, 'row', axis=0, tiled=True)  34.4 us
  transfers between devices with their start and end apart: 2, of which 2 were waited for; matrix products, arithmetic and copies ran while one was open for 0% of the time, Pallas kernels for 0%

profile of v1, /device:TPU:1, one launch (start us, length us, event | category | flops | bytes accessed | tf_op | source)
XLA Modules:
  0.0 1257.2 jit_solution(4493111985102150418)
XLA Ops:
  7.2 52.0 %all_gather.19 = bf16[512,256]{1,0:T(8,128)(2,1)S(1)} all-gather(bf16[32,256]{1,0:T(8,128)(2,1)} %param.14), channel_id=1, replica_groups=mesh['row'=16,'col'=32] {'row'}, dimensions={0}, use_global_device_ids=true | all-gather | bytes 278528 | tf_op jit(solution)/shard_map/all_gather | solution.py:31
  59.3 34.4 %all_gather.18 = bf16[256,256]{1,0:T(8,128)(2,1)S(1)} all-gather(bf16[16,256]{1,0:T(8,128)(2,1)} %param.12), channel_id=1, replica_groups=mesh['row'=16,'col'=32] {'row'}, dimensions={0}, use_global_device_ids=true | all-gather | bytes 139264 | tf_op jit(solution)/shard_map/all_gather | solution.py:30
  93.7 1.5 fusion.16
  95.3 114.2 %all_gather.22 = bf16[256,512]{1,0:T(8,128)(2,1)S(1)} all-gather(bf16[8,512]{1,0:T(8,128)(2,1)S(1)} %copy-done.4), channel_id=1, replica_groups=mesh['row'=16,'col'=32] {'col'}, dimensions={0}, use_global_device_ids=true | all-gather | bytes 270336 | tf_op jit(solution)/shard_map/all_gather | solution.py:34
  209.5 114.3 %all_gather.23 = bf16[512,512]{1,0:T(8,128)(2,1)S(1)} all-gather(bf16[16,512]{1,0:T(8,128)(2,1)S(1)} %copy-done.3), channel_id=1, replica_groups=mesh['row'=16,'col'=32] {'col'}, dimensions={0}, use_global_device_ids=true | all-gather | bytes 540672 | tf_op jit(solution)/shard_map/all_gather | solution.py:35
  323.7 0.4 fusion.12
  324.1 151.8 %all-reduce.4 = bf16[768,256]{1,0:T(8,128)(2,1)S(1)} all-reduce(f32[768,256]{1,0:T(8,128)S(1)} %fusion.12), channel_id=1, replica_groups=mesh['row'=16,'col'=32] {'row'}, use_global_device_ids=true, to_apply=%region_1.0 | all-reduce | flops 196608 | bytes 1179648 | tf_op jit(solution)/shard_map/psum | solution.py:43
  476.6 0.2 copy.20
  476.9 180.1 %all-gather.3.cloned.1.call-done = f32[24576,512]{1,0:T(8,128)} async-done(((f32[768,512]{1,0:T(8,128)}), f32[24576,512]{1,0:T(8,128)}) %all-gather.3.cloned.1.call-update) | async-done | bytes 50331664 | tf_op jit(solution)/shard_map/all_gather | solution.py:12
  657.0 18.0 %reduce_sum.27 = bf16[768,512]{1,0:T(8,128)(2,1)S(1)} reduce(f32[32,768,512]{2,1,0:T(8,128)} %bitcast.41, f32[]{:T(128)} %constant.3.clone.1), dimensions={0}, to_apply=%region_0.0 | reduce | flops 12189696 | bytes 51118084 | tf_op jit(solution)/shard_map/reduce_sum | solution.py:13
  675.1 0.1 copy.19
  675.2 0.5 copy-done.2
  675.7 19.3 %while.10 = (s32[]{:T(128)}, f32[8,4,512]{2,1,0:T(4,128)S(1)}, s32[256]{0:T(256)S(1)}, s32[8]{0:T(128)S(1)}, bf16[256,512]{0,1:T(8,128)(2,1)S(1)}, /*index=5*/bf...) while((s32[]{:T(128)}, f32[8,4,512]{2,1,0:T(4,128)S(1)}, ...), condition=%wide.region_4.5_spmd, body=%wide.region_2.4_spmd.sunk | while | flops 807927808 | bytes 1995937 | solution.py:68
  675.7 0.6 dynamic_slice.10
  676.2 0.6 iota_add_fusion.2
  676.9 0.1 compare_convert_fusion.2
  677.0 1.1 fusion.33
  678.1 0.6 dynamic_slice.10
  678.6 0.6 iota_add_fusion.2
  679.3 0.1 compare_convert_fusion.2
  679.4 1.1 fusion.33
  680.5 0.6 dynamic_slice.10
  681.1 0.6 iota_add_fusion.2
  681.7 0.1 compare_convert_fusion.2
  681.8 1.1 fusion.33
  682.9 0.6 dynamic_slice.10
  683.5 0.6 iota_add_fusion.2
  684.1 0.1 compare_convert_fusion.2
  684.2 1.1 fusion.33
  685.3 0.6 dynamic_slice.10
  685.9 0.6 iota_add_fusion.2
  686.6 0.1 compare_convert_fusion.2
  686.6 1.1 fusion.33
  687.7 0.6 dynamic_slice.10
  688.3 0.6 iota_add_fusion.2
  689.0 1.1 fusion.33
  690.1 0.6 dynamic_slice.10
  690.7 0.6 iota_add_fusion.2
  691.5 1.1 fusion.33
  692.6 0.6 dynamic_slice.10
  693.1 0.6 iota_add_fusion.2
  693.9 1.1 fusion.33
  695.0 0.6 div.26
  695.7 0.1 convert_reduce_fusion
  695.8 551.5 %all-reduce.3.cloned.1.call-done = f32[32,512]{1,0:T(8,128)} async-done(((f32[32,512]{1,0:T(8,128)}), f32[32,512]{1,0:T(8,128)}) %all-reduce.3.cloned.1.call-update) | async-done | bytes 65552 | tf_op jit(solution)/shard_map/psum | solution.py:75
  1247.3 0.8 constant_dynamic-slice_fusion
  1248.1 0.7 copy.21
  1248.8 1.6 convolution_divide_fusion
  (36 shorter events, 0.6 us)
Async XLA Ops:
  7.2 86.5 %copy-start = (bf16[256,512]{1,0:T(8,128)(2,1)S(1)}, bf16[256,512]{1,0:T(8,128)(2,1)}, u32[]{:S(2)}) copy-start(bf16[256,512]{1,0:T(8,128)(2,1)} %param.16) | copy-start | bytes 786436
  7.2 88.1 %copy-start.4 = (bf16[8,512]{1,0:T(8,128)(2,1)S(1)}, bf16[8,512]{1,0:T(8,128)(2,1)}, u32[]{:S(2)}) copy-start(bf16[8,512]{1,0:T(8,128)(2,1)} %param.13) | copy-start | bytes 24580
  7.2 649.8 %all-gather.3.cloned.1.call-start = ((), (), s32[]{:S(2)}) async-start(), calls=%async_computation.1 | async-start | bytes 51904512 | tf_op jit(solution)/shard_map/all_gather | solution.py:12
  59.3 150.2 %copy-start.3 = (bf16[16,512]{1,0:T(8,128)(2,1)S(1)}, bf16[16,512]{1,0:T(8,128)(2,1)}, u32[]{:S(2)}) copy-start(bf16[16,512]{1,0:T(8,128)(2,1)} %param.15) | copy-start | bytes 49156
  93.7 230.1 %copy-start.6 = (bf16[512,256]{1,0:T(8,128)(2,1)S(1)}, bf16[512,256]{1,0:T(8,128)(2,1)}, u32[]{:S(2)}) copy-start(bf16[512,256]{1,0:T(8,128)(2,1)} %param.17) | copy-start | bytes 786436
  95.2 1152.1 %all-reduce.3.cloned.1.call-start = ((), (), s32[]{:S(2)}) async-start(), calls=%async_computation | async-start | bytes 131072 | tf_op jit(solution)/shard_map/psum | solution.py:75
  324.1 152.8 %copy-start.1 = (f32[512,256]{1,0:T(8,128)S(1)}, f32[512,256]{1,0:T(8,128)}, u32[]{:S(2)}) copy-start(f32[512,256]{1,0:T(8,128)} %param.18) | copy-start | bytes 1572868
  675.0 0.7 copy-start.2
  675.7 20.0 %copy-start.5 = (s32[512]{0:T(512)S(1)}, s32[512]{0:T(512)}, u32[]{:S(2)}) copy-start(s32[512]{0:T(512)} %param.21) | copy-start | bytes 6148
Sparse Core Ops, SparseCore 0:
  95.3 561.6 all-gather.2
  695.8 551.4 all-reduce.2
